TPU v7x, 32 devices: a whole 2x2x4 slice. The times are simulated.
32 devices in a mesh: train: 16 (over z, y, core), cand: 2 (over x).
Axes of the slice: x: 2, y: 2, z: 4, core: 2. Of those that a mesh axis runs over, the one named last changes fastest.
Arguments:
- x_train: float32 [8, 2048], P(None, 'train'), may hold values from -4 to 4
- x_cand: float32 [8, 1024], P(None, 'cand'), may hold values from -4 to 4
- targets: float32 [2048], P(('train', 'cand')), may hold values from -6 to 6
- noise: float32 [2048, 64], P(('train', 'cand')), may hold values from -5 to 5
- omega: float32 [8, 4096], replicated, may hold values from -6 to 6
- phase: float32 [4096], replicated, may hold values from -3.140625 to 3.140625
- prior_weights: bfloat16 [4096, 64], P('cand'), may hold values from -6 to 6
Outputs:
- samples: float32 [1024, 64], P(('cand', 'train'))
- solution: float32 [2048, 64], P(('train', 'cand'))
All inputs are finite; a program needn't handle non-finite values.
Results may differ from a plain program's by a relative error of at most 0.0019.
The roundings to bfloat16 on the way count: a program that leaves them out, or rounds other values in their place, can miss the bound.
Values may be sent and summed in bfloat16 or wider, within the bound.
No kernel may reach another device: no remote copies, remote signals or barrier semaphores. Data moves between devices by JAX's collectives and lax.ppermute only.
A program may use at most 64 MiB of HBM per device.

v0:
```python
import math
import jax
import jax.numpy as jnp
from jax import lax
from jax.sharding import PartitionSpec as P

ITERS = 2
noise_level = 0.5


def squares_of(points):
    return jnp.sum(points * points, axis=0)


def kernel_tile(row_points, row_norms, column_points, column_norms):
    inner = jnp.dot(row_points.T, column_points, precision=lax.Precision.HIGHEST)
    return jnp.exp(-0.5 * (row_norms[:, None] + column_norms[None, :] - 2.0 * inner)).astype(
        jnp.bfloat16
    )


def features(points, omega, phase):
    angles = jnp.dot(points.T, omega, precision=lax.Precision.HIGHEST) + phase[None, :]
    return (math.sqrt(2.0 / omega.shape[1]) * jnp.cos(angles)).astype(jnp.bfloat16)


def kernel_rows(points, every_point, every_norm, weights):
    count = points.shape[1]
    size = math.gcd(count, 1024)
    stacked = points.reshape(points.shape[0], count // size, size).transpose(1, 0, 2)

    def one_block(block_points):
        tile = kernel_tile(block_points, squares_of(block_points), every_point, every_norm)
        return jnp.dot(tile, weights, preferred_element_type=jnp.float32)

    return lax.map(one_block, stacked).reshape(count, weights.shape[1])


def body(x_train, x_cand, targets, noise, omega, phase, prior_weights):
    own_rows = noise.shape[0]
    cand_index = lax.axis_index("cand")
    train_index = lax.axis_index("train")
    own_points = lax.dynamic_slice_in_dim(x_train, cand_index * own_rows, own_rows, 1)
    full_weights = lax.all_gather(prior_weights, "cand", axis=0, tiled=True)
    prior_train = jnp.dot(
        features(own_points, omega, phase), full_weights, preferred_element_type=jnp.float32
    )
    rhs = targets[:, None] - prior_train - noise
    column_points = lax.all_gather(own_points, "train", axis=1, tiled=True)
    row_norms = squares_of(x_train)
    column_norms = squares_of(column_points)
    width = max(128, 262144 // x_train.shape[1])

    def squares(values):
        return lax.psum(jnp.sum(values * values, axis=0), ("train", "cand"))

    solution = jnp.zeros(rhs.shape, jnp.float32)
    residual = rhs
    direction = rhs
    norm_now = squares(residual)
    for step in range(ITERS):
        packed = direction.astype(jnp.bfloat16)
        empty = jnp.zeros((x_train.shape[1], packed.shape[1]), jnp.float32)
        total = empty
        piece = lax.all_gather(packed, "train", axis=0, tiled=True)
        for offset in range(0, piece.shape[0], width):
            count = min(width, piece.shape[0] - offset)
            accumulate_points = lax.dynamic_slice_in_dim(column_points, offset, count, 1)
            norms = lax.dynamic_slice_in_dim(column_norms, offset, count, 0)
            tile = kernel_tile(x_train, row_norms, accumulate_points, norms)
            total = total + jnp.dot(
                tile, piece[offset : offset + count], preferred_element_type=jnp.float32
            )
        apply_total = total
        apply_total = lax.psum_scatter(apply_total, "cand", scatter_dimension=0, tiled=True)
        image = apply_total + noise_level * direction
        curve = lax.psum(jnp.sum(direction * image, axis=0), ("train", "cand"))
        alpha = norm_now / curve
        solution = solution + alpha * direction
        residual = residual - alpha * image
        norm_next = squares(residual)
        direction = residual + norm_next / norm_now * direction
        norm_now = norm_next
    per_device = x_cand.shape[1] // lax.axis_size("train")
    mine = lax.dynamic_slice_in_dim(x_cand, train_index * per_device, per_device, 1)
    packed_solution = solution.astype(jnp.bfloat16)
    block_weights = lax.all_gather(packed_solution, "cand", axis=0, tiled=True)
    train_norms = squares_of(x_train)
    kernel_part = lax.psum_scatter(
        kernel_rows(x_cand, x_train, train_norms, block_weights),
        "train",
        scatter_dimension=0,
        tiled=True,
    )
    prior_cand = jnp.dot(
        features(mine, omega, phase), full_weights, preferred_element_type=jnp.float32
    )
    return (prior_cand + kernel_part, solution)


def solution(mesh):
    placed = (
        P(None, "train"),
        P(None, "cand"),
        P(("train", "cand")),
        P(("train", "cand"), None),
        P(),
        P(),
        P("cand", None),
    )
    return jax.shard_map(
        body,
        mesh=mesh,
        in_specs=placed,
        out_specs=(P(("cand", "train"), None), P(("train", "cand"), None)),
        check_vma=False,
    )
```

profile of v0, /device:TPU:0, one launch (start us, length us, event | category | flops | bytes accessed | tf_op | source)
XLA Modules:
  0.0 296.1 jit_solution(272035158380049314)
XLA Ops:
  7.2 0.0 copy-start
  7.2 0.0 reduce-scatter.4.cloned.1.call-start
  7.2 0.7 multiply_reduce_fusion.6
  8.0 0.0 copy-start.3
  8.0 10.3 %all_gather.15 = bf16[4096,64]{0,1:T(8,128)(2,1)S(1)} all-gather(bf16[2048,64]{0,1:T(8,128)(2,1)} %param.13), channel_id=1, replica_groups=mesh['train'=16,'cand'=2] {'cand'}, dimensions={0}, use_global_device_ids=true | all-gather | bytes 786432 | tf_op jit(solution)/shard_map/all_gather | solution.py:44
  18.3 0.0 copy-done.3
  18.3 0.1 dynamic-slice_bitcast_fusion
  18.4 22.0 %all-gather = f32[16,64,8]{1,2,0:T(8,128)S(1)} all-gather(f32[1,64,8]{1,2,0:T(8,128)S(1)} %dynamic-slice_bitcast_fusion), channel_id=1, replica_groups=mesh['train'=16,'cand'=2] {'train'}, dimensions={0}, use_global_device_ids=true | all-gather | bytes 34816 | tf_op jit(solution)/shard_map/all_gather | solution.py:49
  40.4 0.1 reshape.18
  40.5 0.0 copy-start.2
  40.5 0.0 copy-done
  40.5 0.7 copy-done.2
  41.2 0.0 copy-start.4
  41.2 0.0 copy-start.6
  41.2 4.7 %fusion.2 = bf16[64,4096]{1,0:T(8,128)(2,1)S(1)} fusion(f32[8,4096]{1,0:T(8,128)S(1)} %copy-done, f32[4096]{0:T(1024)S(1)} %copy-done.2, f32[8,128]{1,0:T(8,128)S(1)} %copy-done.3, s32[]{:T(128)S(6)} %select_n.7), kind=kOutput, calls=%fused_computation.3 | convolution fusion | flops 25952256 | bytes 675844 | tf_op jit(solution)/shard_map/dot_general | solution.py:23
  45.9 0.0 copy-done.4
  45.9 0.0 copy-done.6
  46.0 0.3 fusion.22
  46.3 18.1 %all_gather.17 = bf16[1024,64]{1,0:T(8,128)(2,1)S(1)} all-gather(bf16[64,64]{1,0:T(8,128)(2,1)S(1)} %get-tuple-element.26), channel_id=1, replica_groups=mesh['train'=16,'cand'=2] {'train'}, dimensions={0}, use_global_device_ids=true | all-gather | bytes 139264 | tf_op jit(solution)/shard_map/all_gather | solution.py:65
  64.4 1.0 fusion.10
  65.5 0.9 fusion.23
  66.4 0.0 copy-start.5
  66.4 0.0 reduce-scatter.4.cloned.1.call-update
  66.4 0.0 reduce-scatter.6.cloned.1.call-start
  66.5 0.6 copy-done.5
  67.1 7.8 %reduce-scatter.4.cloned.1.call-done = f32[64,64]{1,0:T(8,128)} async-done(((f32[128,64]{1,0:T(8,128)}), f32[64,64]{1,0:T(8,128)}) %reduce-scatter.4.cloned.1.call-update) | async-done | bytes 16400 | tf_op jit(solution)/shard_map/reduce_scatter | solution.py:75
  74.9 0.0 copy-start.1
  74.9 0.9 multiply_reduce_fusion.3
  75.8 39.3 %all-reduce = (f32[64]{0:T(128)S(1)}, f32[64]{0:T(128)S(1)}) all-reduce(f32[64]{0:T(128)S(1)} %get-tuple-element.15, f32[64]{0:T(128)S(1)} %get-tuple-element.14), channel_id=1, replica_groups=mesh['train'=16,'cand'=2] {'train','cand'}, use_global_device_ids=true, to_apply=%region_3.0 | all-reduce | flops 128 | bytes 1024 | tf_op jit(solution)/shard_map/psum | solution.py:55
  115.1 0.0 copy-done.1
  115.2 41.0 %psum.30 = f32[64]{0:T(128)S(1)} all-reduce(f32[64]{0:T(128)S(1)} %multiply_reduce_fusion.2), channel_id=1, replica_groups=mesh['train'=16,'cand'=2] {'train','cand'}, use_global_device_ids=true, to_apply=%region_9.0 | all-reduce | flops 64 | bytes 512 | tf_op jit(solution)/shard_map/psum | solution.py:55
  156.2 21.8 %all_gather.18 = bf16[1024,64]{1,0:T(8,128)(2,1)S(1)} all-gather(bf16[64,64]{1,0:T(8,128)(2,1)S(1)} %fusion.20), channel_id=1, replica_groups=mesh['train'=16,'cand'=2] {'train'}, dimensions={0}, use_global_device_ids=true | all-gather | bytes 139264 | tf_op jit(solution)/shard_map/all_gather | solution.py:65
  178.0 0.9 fusion.24
  178.9 0.0 reduce-scatter.6.cloned.1.call-update
  178.9 0.0 reduce-scatter.8.cloned.1.call-start
  178.9 0.6 fusion.14
  179.6 5.8 %reduce-scatter.6.cloned.1.call-done = f32[64,64]{1,0:T(8,128)} async-done(((f32[128,64]{1,0:T(8,128)}), f32[64,64]{1,0:T(8,128)}) %reduce-scatter.6.cloned.1.call-update) | async-done | bytes 16400 | tf_op jit(solution)/shard_map/reduce_scatter | solution.py:75
  185.4 0.8 multiply_reduce_fusion.1
  186.1 39.3 %psum.31 = f32[64]{0:T(128)S(1)} all-reduce(f32[64]{0:T(128)S(1)} %multiply_reduce_fusion.1), channel_id=1, replica_groups=mesh['train'=16,'cand'=2] {'train','cand'}, use_global_device_ids=true, to_apply=%region_12.0 | all-reduce | flops 64 | bytes 512 | tf_op jit(solution)/shard_map/psum | solution.py:77
  225.5 0.6 fusion.21
  226.1 4.6 %all_gather.19 = bf16[128,64]{1,0:T(8,128)(2,1)S(1)} all-gather(bf16[64,64]{1,0:T(8,128)(2,1)S(1)} %get-tuple-element.24), channel_id=1, replica_groups=mesh['train'=16,'cand'=2] {'cand'}, dimensions={0}, use_global_device_ids=true | all-gather | bytes 24576 | tf_op jit(solution)/shard_map/all_gather | solution.py:87
  230.7 0.9 fusion.25
  231.6 0.0 reduce-scatter.8.cloned.1.call-update
  231.6 2.7 fusion.5
  234.3 53.7 %reduce-scatter.8.cloned.1.call-done = f32[32,64]{1,0:T(8,128)} async-done(((f32[512,64]{1,0:T(8,128)}), f32[32,64]{1,0:T(8,128)}) %reduce-scatter.8.cloned.1.call-update) | async-done | bytes 8208 | tf_op jit(solution)/shard_map/reduce_scatter | solution.py:89
  288.0 1.6 convolution_add_fusion.2
  (8 shorter events, 0.1 us)
Async XLA Ops:
  7.2 33.3 %copy-start = (f32[8,4096]{1,0:T(8,128)S(1)}, f32[8,4096]{1,0:T(8,128)}, u32[]{:S(2)}) copy-start(f32[8,4096]{1,0:T(8,128)} %param.11) | copy-start | bytes 393220
  7.2 67.8 %reduce-scatter.4.cloned.1.call-start = ((), (), s32[]{:S(2)}) async-start(), calls=%async_computation.3 | async-start | bytes 98304 | tf_op jit(solution)/shard_map/reduce_scatter | solution.py:75
  8.0 10.3 %copy-start.3 = (f32[8,128]{1,0:T(8,128)S(1)}, f32[8,128]{1,0:T(8,128)}, u32[]{:S(2)}) copy-start(f32[8,128]{1,0:T(8,128)} %param.7) | copy-start | bytes 12292
  40.5 0.7 copy-start.2
  41.2 4.8 %copy-start.4 = (f32[64,64]{1,0:T(8,128)S(1)}, f32[64,64]{1,0:T(8,128)}, u32[]{:S(2)}) copy-start(f32[64,64]{1,0:T(8,128)} %param.10) | copy-start | bytes 49156
  41.2 4.8 %copy-start.6 = (f32[64]{0:T(128)S(1)}, f32[64]{0:T(128)}, u32[]{:S(2)}) copy-start(f32[64]{0:T(128)} %param.9) | copy-start | bytes 772
  66.4 0.7 copy-start.5
  66.4 119.0 %reduce-scatter.6.cloned.1.call-start = ((), (), s32[]{:S(2)}) async-start(), calls=%async_computation.4 | async-start | bytes 98304 | tf_op jit(solution)/shard_map/reduce_scatter | solution.py:75
  74.9 40.2 %copy-start.1 = (f32[64,64]{1,0:T(8,128)S(1)}, f32[64,64]{1,0:T(8,128)}, u32[]{:S(2)}) copy-start(f32[64,64]{1,0:T(8,128)} %reduce-scatter.4.cloned.1.call-done) | copy-start | bytes 49156
  178.9 109.1 %reduce-scatter.8.cloned.1.call-start = ((), (), s32[]{:S(2)}) async-start(), calls=%async_computation.5 | async-start | bytes 278528 | tf_op jit(solution)/shard_map/reduce_scatter | solution.py:89
Sparse Core Ops, SparseCore 0:
  66.5 8.3 reduce-scatter.3
  179.0 6.2 reduce-scatter.5
  231.8 56.2 reduce-scatter.7
where the time goes:
time: 297 us; the launch traced here: 296 us
  blocking collectives  197 us (66%)
  waiting for transfers between devices  67.3 us (23%)
  between operations  13.9 us (5%)
  matrix products  13.6 us (5%)
  other arithmetic  3.1 us (1%)
    psum x2, blocking collectives, squares(): return lax.psum(jnp.sum(values * values, axis=0), ('train', 'cand'))  80.3 us
    reduce_scatter x1, waiting for transfers between devices, body(): lax.psum_scatter(kernel_rows(x_cand, x_train, train_norms, block_weights)...  53.7 us
    all_gather x2, blocking collectives, body(): piece = lax.all_gather(packed, 'train', axis=0, tiled=True)  40 us
    psum x1, blocking collectives, body(): curve = lax.psum(jnp.sum(direction * image, axis=0), ('train', 'cand'))  39.3 us
    all_gather x1, blocking collectives, body(): column_points = lax.all_gather(own_points, 'train', axis=1, tiled=True)  22 us
    reduce_scatter x2, waiting for transfers between devices, body(): lax.psum_scatter(apply_total, 'cand', scatter_dimension=0, tiled=True)  13.6 us
    all_gather x1, blocking collectives, body(): full_weights = lax.all_gather(prior_weights, 'cand', axis=0, tiled=True)  10.3 us
    dot_general x2, matrix products, features(): jnp.dot(points.T, omega, precision=lax.Precision.HIGHEST) + phase[None, :]  7.44 us
  transfers between devices with their start and end apart: 3, of which 3 were waited for; matrix products, arithmetic and copies ran while one was open for 1% of the time, Pallas kernels for 0%

commit v1 on v0

--- a/solution.py
+++ b/solution.py
@@ -46,7 +46,22 @@
         features(own_points, omega, phase), full_weights, preferred_element_type=jnp.float32
     )
     rhs = targets[:, None] - prior_train - noise
-    column_points = lax.all_gather(own_points, "train", axis=1, tiled=True)
+
+    def step_on_set(field):
+        size_here = lax.axis_size("train")
+        samples = list(map(lambda to_i: (to_i, (to_i + 1) % size_here), range(size_here)))
+        pool = list(map(lambda to_i: (to_i, (to_i - 1) % size_here), range(size_here)))
+        top, a_next = ([field], [field])
+        for _ in range(size_here // 2):
+            top.append(lax.ppermute(top[-1], axis_name="train", perm=samples))
+        for _ in range((size_here - 1) // 2):
+            a_next.append(lax.ppermute(a_next[-1], axis_name="train", perm=pool))
+        local_part = jnp.concatenate([*top[::-1], *a_next[1:]], axis=1)
+        return jnp.roll(
+            local_part, (lax.axis_index("train") - size_here // 2) * field.shape[1], axis=1
+        )
+
+    column_points = step_on_set(own_points)
     row_norms = squares_of(x_train)
     column_norms = squares_of(column_points)
     width = max(128, 262144 // x_train.shape[1])

time: 297 us -> 309 us (1.040)
  starting transfers between devices: 0.12 us -> 31.2 us
  blocking collectives: 197 us -> 172 us
  waiting for transfers between devices: 67.3 us -> 73.3 us
    ppermute x0 -> x15, starting transfers between devices: none -> 31.1 us  [the longest x7 30.5 us: step_on_set(): a_next.append(lax.ppermute(a_next[-1], axis_name='train', perm=pool))]
    all_gather x1 -> x0, blocking collectives: 22 us -> none  [body(): column_points = lax.all_gather(own_points, 'train', axis=1, tiled=True)]
    ppermute x0 -> x15, waiting for transfers between devices: none -> 6.22 us  [the longest x8 3.86 us: step_on_set(): top.append(lax.ppermute(top[-1], axis_name='train', perm=samples))]
    all_gather x1, blocking collectives: 10.3 us -> 7.04 us  [body(): full_weights = lax.all_gather(prior_weights, 'cand', axis=0, tiled=True)]
  transfers between devices with their start and end apart: 3 -> 18, of which waited for: 3 -> 8; matrix products, arithmetic and copies ran while one was open for 1% -> 3% of each run, Pallas kernels for 0% -> 0%
where the time goes in v1:
time: 309 us; the launch traced here: 308 us
  blocking collectives  172 us (56%)
  waiting for transfers between devices  73.3 us (24%)
  starting transfers between devices  31.2 us (10%)
  between operations  13.9 us (4%)
  matrix products  13.6 us (4%)
    psum x2, blocking collectives, squares(): return lax.psum(jnp.sum(values * values, axis=0), ('train', 'cand'))  80.3 us
    reduce_scatter x1, waiting for transfers between devices, body(): lax.psum_scatter(kernel_rows(x_cand, x_train, train_norms, block_weights)...  53.7 us
    all_gather x2, blocking collectives, body(): piece = lax.all_gather(packed, 'train', axis=0, tiled=True)  40.6 us
    psum x1, blocking collectives, body(): curve = lax.psum(jnp.sum(direction * image, axis=0), ('train', 'cand'))  39.3 us
    ppermute x7, starting transfers between devices, step_on_set(): a_next.append(lax.ppermute(a_next[-1], axis_name='train', perm=pool))  30.5 us
    reduce_scatter x2, waiting for transfers between devices, body(): lax.psum_scatter(apply_total, 'cand', scatter_dimension=0, tiled=True)  13.3 us
    dot_general x2, matrix products, features(): jnp.dot(points.T, omega, precision=lax.Precision.HIGHEST) + phase[None, :]  7.32 us
    all_gather x1, blocking collectives, body(): full_weights = lax.all_gather(prior_weights, 'cand', axis=0, tiled=True)  7.04 us
  transfers between devices with their start and end apart: 18, of which 8 were waited for; matrix products, arithmetic and copies ran while one was open for 3% of the time, Pallas kernels for 0%

profile of v1, /device:TPU:0, one launch (start us, length us, event | category | flops | bytes accessed | tf_op | source)
XLA Modules:
  0.0 307.9 jit_solution(14169376286104838684)
XLA Ops:
  7.2 0.0 copy-start
  7.2 0.0 reduce-scatter.4.cloned.1.call-start
  7.2 0.8 constant_dynamic-slice_fusion
  8.0 0.5 collective-permute-start
  8.5 5.0 %collective-permute-start.8 = (f32[8,64]{1,0:T(8,128)S(1)}, f32[8,64]{1,0:T(8,128)S(1)}, u32[]{:S(2)}, u32[]{:S(2)}) collective-permute-start(f32[8,64]{1,0:T(8,128)S(1)} %constant_dynamic-slice_fusion), channel_id=1, source_target_pairs={{0,30},{2,0},{4,2},{6,4},{8,6},{10,8},{12,10},{14,12},{16,14},{18,... | collective-permute-start | bytes 6152 | tf_op jit(solution)/shard_map/ppermute | solution.py:58
  13.5 1.3 collective-permute-done
  14.8 0.0 collective-permute-start.1
  14.8 0.0 collective-permute-done.8
  14.8 4.4 %collective-permute-start.9 = (f32[8,64]{1,0:T(8,128)S(1)}, f32[8,64]{1,0:T(8,128)S(1)}, u32[]{:S(2)}, u32[]{:S(2)}) collective-permute-start(f32[8,64]{1,0:T(8,128)S(1)} %collective-permute-done.8), channel_id=1, source_target_pairs={{0,30},{2,0},{4,2},{6,4},{8,6},{10,8},{12,10},{14,12},{16,14},{18,... | collective-permute-start | bytes 6152 | tf_op jit(solution)/shard_map/ppermute | solution.py:58
  19.2 1.3 collective-permute-done.1
  20.5 0.0 collective-permute-start.2
  20.5 0.0 collective-permute-done.9
  20.5 4.4 %collective-permute-start.10 = (f32[8,64]{1,0:T(8,128)S(1)}, f32[8,64]{1,0:T(8,128)S(1)}, u32[]{:S(2)}, u32[]{:S(2)}) collective-permute-start(f32[8,64]{1,0:T(8,128)S(1)} %collective-permute-done.9), channel_id=1, source_target_pairs={{0,30},{2,0},{4,2},{6,4},{8,6},{10,8},{12,10},{14,12},{16,14},{18,... | collective-permute-start | bytes 6152 | tf_op jit(solution)/shard_map/ppermute | solution.py:58
  24.9 1.3 collective-permute-done.2
  26.2 0.0 collective-permute-start.3
  26.2 4.6 %fusion.2 = bf16[64,4096]{1,0:T(8,128)(2,1)S(1)} fusion(f32[8,64]{1,0:T(8,128)S(1)} %constant_dynamic-slice_fusion, f32[8,4096]{1,0:T(8,128)S(1)} %copy-done, f32[4096]{0:T(1024)S(1)} %copy-done.3), kind=kOutput, calls=%fused_computation.3 | convolution fusion | flops 25952256 | bytes 673792 | tf_op jit(solution)/shard_map/dot_general | solution.py:23
  30.9 0.0 copy-start.4
  30.9 0.0 copy-start.7
  30.9 0.0 collective-permute-done.10
  30.9 4.5 %collective-permute-start.11 = (f32[8,64]{1,0:T(8,128)S(1)}, f32[8,64]{1,0:T(8,128)S(1)}, u32[]{:S(2)}, u32[]{:S(2)}) collective-permute-start(f32[8,64]{1,0:T(8,128)S(1)} %collective-permute-done.10), channel_id=1, source_target_pairs={{0,30},{2,0},{4,2},{6,4},{8,6},{10,8},{12,10},{14,12},{16,14},{18,... | collective-permute-start | bytes 6152 | tf_op jit(solution)/shard_map/ppermute | solution.py:58
  35.4 0.0 collective-permute-done.3
  35.4 0.0 collective-permute-start.4
  35.4 7.0 %all_gather.12 = bf16[4096,64]{0,1:T(8,128)(2,1)S(1)} all-gather(bf16[2048,64]{0,1:T(8,128)(2,1)S(1)} %copy-done.2), channel_id=1, replica_groups=mesh['train'=16,'cand'=2] {'cand'}, dimensions={0}, use_global_device_ids=true | all-gather | bytes 786432 | tf_op jit(solution)/shard_map/all_gather | solution.py:44
  42.4 0.0 collective-permute-done.11
  42.4 3.5 %collective-permute-start.12 = (f32[8,64]{1,0:T(8,128)S(1)}, f32[8,64]{1,0:T(8,128)S(1)}, u32[]{:S(2)}, u32[]{:S(2)}) collective-permute-start(f32[8,64]{1,0:T(8,128)S(1)} %collective-permute-done.11), channel_id=1, source_target_pairs={{0,30},{2,0},{4,2},{6,4},{8,6},{10,8},{12,10},{14,12},{16,14},{18,... | collective-permute-start | bytes 6152 | tf_op jit(solution)/shard_map/ppermute | solution.py:58
  45.9 0.0 collective-permute-done.4
  45.9 0.0 collective-permute-start.5
  45.9 0.3 fusion.22
  46.3 1.0 collective-permute-done.12
  47.2 4.4 %collective-permute-start.13 = (f32[8,64]{1,0:T(8,128)S(1)}, f32[8,64]{1,0:T(8,128)S(1)}, u32[]{:S(2)}, u32[]{:S(2)}) collective-permute-start(f32[8,64]{1,0:T(8,128)S(1)} %collective-permute-done.12), channel_id=1, source_target_pairs={{0,30},{2,0},{4,2},{6,4},{8,6},{10,8},{12,10},{14,12},{16,14},{18,... | collective-permute-start | bytes 6152 | tf_op jit(solution)/shard_map/ppermute | solution.py:58
  51.6 0.0 collective-permute-done.5
  51.6 0.0 collective-permute-start.6
  51.7 1.3 collective-permute-done.13
  53.0 4.4 %collective-permute-start.14 = (f32[8,64]{1,0:T(8,128)S(1)}, f32[8,64]{1,0:T(8,128)S(1)}, u32[]{:S(2)}, u32[]{:S(2)}) collective-permute-start(f32[8,64]{1,0:T(8,128)S(1)} %collective-permute-done.13), channel_id=1, source_target_pairs={{0,30},{2,0},{4,2},{6,4},{8,6},{10,8},{12,10},{14,12},{16,14},{18,... | collective-permute-start | bytes 6152 | tf_op jit(solution)/shard_map/ppermute | solution.py:58
  57.4 0.0 collective-permute-done.6
  57.4 0.0 collective-permute-start.7
  57.4 18.8 %all_gather.13 = bf16[1024,64]{1,0:T(8,128)(2,1)S(1)} all-gather(bf16[64,64]{1,0:T(8,128)(2,1)S(1)} %get-tuple-element.26), channel_id=1, replica_groups=mesh['train'=16,'cand'=2] {'train'}, dimensions={0}, use_global_device_ids=true | all-gather | bytes 139264 | tf_op jit(solution)/shard_map/all_gather | solution.py:80
  76.2 0.0 collective-permute-done.14
  76.2 0.1 concatenate.6
  76.3 0.1 multiply_reduce_fusion.3
  76.4 1.1 fusion.10
  77.5 0.9 fusion.23
  78.4 0.0 reduce-scatter.4.cloned.1.call-update
  78.4 0.0 reduce-scatter.6.cloned.1.call-start
  78.5 0.6 copy-done.5
  79.1 7.5 %reduce-scatter.4.cloned.1.call-done = f32[64,64]{1,0:T(8,128)} async-done(((f32[128,64]{1,0:T(8,128)}), f32[64,64]{1,0:T(8,128)}) %reduce-scatter.4.cloned.1.call-update) | async-done | bytes 16400 | tf_op jit(solution)/shard_map/reduce_scatter | solution.py:90
  86.7 0.9 multiply_reduce_fusion.2
  87.5 39.3 %all-reduce = (f32[64]{0:T(128)S(1)}, f32[64]{0:T(128)S(1)}) all-reduce(f32[64]{0:T(128)S(1)} %get-tuple-element.15, f32[64]{0:T(128)S(1)} %get-tuple-element.14), channel_id=1, replica_groups=mesh['train'=16,'cand'=2] {'train','cand'}, use_global_device_ids=true, to_apply=%region_3.4 | all-reduce | flops 128 | bytes 1024 | tf_op jit(solution)/shard_map/psum | solution.py:70
  126.9 41.0 %psum.30 = f32[64]{0:T(128)S(1)} all-reduce(f32[64]{0:T(128)S(1)} %multiply_reduce_fusion.1), channel_id=1, replica_groups=mesh['train'=16,'cand'=2] {'train','cand'}, use_global_device_ids=true, to_apply=%region_9.10 | all-reduce | flops 64 | bytes 512 | tf_op jit(solution)/shard_map/psum | solution.py:70
  167.9 21.8 %all_gather.14 = bf16[1024,64]{1,0:T(8,128)(2,1)S(1)} all-gather(bf16[64,64]{1,0:T(8,128)(2,1)S(1)} %fusion.20), channel_id=1, replica_groups=mesh['train'=16,'cand'=2] {'train'}, dimensions={0}, use_global_device_ids=true | all-gather | bytes 139264 | tf_op jit(solution)/shard_map/all_gather | solution.py:80
  189.7 0.9 fusion.24
  190.6 0.0 reduce-scatter.6.cloned.1.call-update
  190.6 0.0 reduce-scatter.8.cloned.1.call-start
  190.7 0.6 fusion.14
  191.3 5.8 %reduce-scatter.6.cloned.1.call-done = f32[64,64]{1,0:T(8,128)} async-done(((f32[128,64]{1,0:T(8,128)}), f32[64,64]{1,0:T(8,128)}) %reduce-scatter.6.cloned.1.call-update) | async-done | bytes 16400 | tf_op jit(solution)/shard_map/reduce_scatter | solution.py:90
  197.1 0.8 multiply_reduce_fusion
  197.9 39.3 %psum.31 = f32[64]{0:T(128)S(1)} all-reduce(f32[64]{0:T(128)S(1)} %multiply_reduce_fusion), channel_id=1, replica_groups=mesh['train'=16,'cand'=2] {'train','cand'}, use_global_device_ids=true, to_apply=%region_12.13 | all-reduce | flops 64 | bytes 512 | tf_op jit(solution)/shard_map/psum | solution.py:92
  237.2 0.6 fusion.21
  237.8 4.6 %all_gather.15 = bf16[128,64]{1,0:T(8,128)(2,1)S(1)} all-gather(bf16[64,64]{1,0:T(8,128)(2,1)S(1)} %get-tuple-element.24), channel_id=1, replica_groups=mesh['train'=16,'cand'=2] {'cand'}, dimensions={0}, use_global_device_ids=true | all-gather | bytes 24576 | tf_op jit(solution)/shard_map/all_gather | solution.py:102
  242.4 0.9 fusion.25
  243.3 0.0 reduce-scatter.8.cloned.1.call-update
  243.3 2.7 fusion.5
  246.0 53.7 %reduce-scatter.8.cloned.1.call-done = f32[32,64]{1,0:T(8,128)} async-done(((f32[512,64]{1,0:T(8,128)}), f32[32,64]{1,0:T(8,128)}) %reduce-scatter.8.cloned.1.call-update) | async-done | bytes 8208 | tf_op jit(solution)/shard_map/reduce_scatter | solution.py:104
  299.8 1.6 convolution_add_fusion.2
  (20 shorter events, 0.1 us)
Async XLA Ops:
  7.2 19.1 %copy-start = (f32[8,4096]{1,0:T(8,128)S(1)}, f32[8,4096]{1,0:T(8,128)}, u32[]{:S(2)}) copy-start(f32[8,4096]{1,0:T(8,128)} %param.11) | copy-start | bytes 393220
  7.2 19.1 %copy-start.3 = (f32[4096]{0:T(1024)S(1)}, f32[4096]{0:T(1024)}, u32[]{:S(2)}) copy-start(f32[4096]{0:T(1024)} %param.12) | copy-start | bytes 49156
  7.2 79.5 %reduce-scatter.4.cloned.1.call-start = ((), (), s32[]{:S(2)}) async-start(), calls=%async_computation.3 | async-start | bytes 98304 | tf_op jit(solution)/shard_map/reduce_scatter | solution.py:90
  8.0 27.4 %copy-start.2 = (bf16[2048,64]{0,1:T(8,128)(2,1)S(1)}, bf16[2048,64]{0,1:T(8,128)(2,1)}, u32[]{:S(2)}) copy-start(bf16[2048,64]{0,1:T(8,128)(2,1)} %param.13) | copy-start | bytes 786436
  8.0 6.8 %collective-permute-start = (f32[8,64]{1,0:T(8,128)S(1)}, f32[8,64]{1,0:T(8,128)S(1)}, u32[]{:S(2)}, u32[]{:S(2)}) collective-permute-start(f32[8,64]{1,0:T(8,128)S(1)} %constant_dynamic-slice_fusion), channel_id=1, source_target_pairs={{0,2},{2,4},{4,6},{6,8},{8,10},{10,12},{12,14},{14,16},{16,18},{18... | collective-permute-start | bytes 6152 | tf_op jit(solution)/shard_map/ppermute | solution.py:56
  8.5 6.3 %collective-permute-start.8 = (f32[8,64]{1,0:T(8,128)S(1)}, f32[8,64]{1,0:T(8,128)S(1)}, u32[]{:S(2)}, u32[]{:S(2)}) collective-permute-start(f32[8,64]{1,0:T(8,128)S(1)} %constant_dynamic-slice_fusion), channel_id=1, source_target_pairs={{0,30},{2,0},{4,2},{6,4},{8,6},{10,8},{12,10},{14,12},{16,14},{18,... | collective-permute-start | bytes 6152 | tf_op jit(solution)/shard_map/ppermute | solution.py:58
  14.8 5.7 %collective-permute-start.1 = (f32[8,64]{1,0:T(8,128)S(1)}, f32[8,64]{1,0:T(8,128)S(1)}, u32[]{:S(2)}, u32[]{:S(2)}) collective-permute-start(f32[8,64]{1,0:T(8,128)S(1)} %collective-permute-done), channel_id=1, source_target_pairs={{0,2},{2,4},{4,6},{6,8},{8,10},{10,12},{12,14},{14,16},{16,18},{18... | collective-permute-start | bytes 6152 | tf_op jit(solution)/shard_map/ppermute | solution.py:56
  14.8 5.7 %collective-permute-start.9 = (f32[8,64]{1,0:T(8,128)S(1)}, f32[8,64]{1,0:T(8,128)S(1)}, u32[]{:S(2)}, u32[]{:S(2)}) collective-permute-start(f32[8,64]{1,0:T(8,128)S(1)} %collective-permute-done.8), channel_id=1, source_target_pairs={{0,30},{2,0},{4,2},{6,4},{8,6},{10,8},{12,10},{14,12},{16,14},{18,... | collective-permute-start | bytes 6152 | tf_op jit(solution)/shard_map/ppermute | solution.py:58
  20.5 5.7 %collective-permute-start.2 = (f32[8,64]{1,0:T(8,128)S(1)}, f32[8,64]{1,0:T(8,128)S(1)}, u32[]{:S(2)}, u32[]{:S(2)}) collective-permute-start(f32[8,64]{1,0:T(8,128)S(1)} %collective-permute-done.1), channel_id=1, source_target_pairs={{0,2},{2,4},{4,6},{6,8},{8,10},{10,12},{12,14},{14,16},{16,18},{18... | collective-permute-start | bytes 6152 | tf_op jit(solution)/shard_map/ppermute | solution.py:56
  20.5 10.3 %collective-permute-start.10 = (f32[8,64]{1,0:T(8,128)S(1)}, f32[8,64]{1,0:T(8,128)S(1)}, u32[]{:S(2)}, u32[]{:S(2)}) collective-permute-start(f32[8,64]{1,0:T(8,128)S(1)} %collective-permute-done.9), channel_id=1, source_target_pairs={{0,30},{2,0},{4,2},{6,4},{8,6},{10,8},{12,10},{14,12},{16,14},{18,... | collective-permute-start | bytes 6152 | tf_op jit(solution)/shard_map/ppermute | solution.py:58
  26.2 9.1 %collective-permute-start.3 = (f32[8,64]{1,0:T(8,128)S(1)}, f32[8,64]{1,0:T(8,128)S(1)}, u32[]{:S(2)}, u32[]{:S(2)}) collective-permute-start(f32[8,64]{1,0:T(8,128)S(1)} %collective-permute-done.2), channel_id=1, source_target_pairs={{0,2},{2,4},{4,6},{6,8},{8,10},{10,12},{12,14},{14,16},{16,18},{18... | collective-permute-start | bytes 6152 | tf_op jit(solution)/shard_map/ppermute | solution.py:56
  30.9 15.1 %copy-start.4 = (f32[64,64]{1,0:T(8,128)S(1)}, f32[64,64]{1,0:T(8,128)}, u32[]{:S(2)}) copy-start(f32[64,64]{1,0:T(8,128)} %param.10) | copy-start | bytes 49156
  30.9 15.0 %copy-start.7 = (f32[64]{0:T(128)S(1)}, f32[64]{0:T(128)}, u32[]{:S(2)}) copy-start(f32[64]{0:T(128)} %param.9) | copy-start | bytes 772
  30.9 11.5 %collective-permute-start.11 = (f32[8,64]{1,0:T(8,128)S(1)}, f32[8,64]{1,0:T(8,128)S(1)}, u32[]{:S(2)}, u32[]{:S(2)}) collective-permute-start(f32[8,64]{1,0:T(8,128)S(1)} %collective-permute-done.10), channel_id=1, source_target_pairs={{0,30},{2,0},{4,2},{6,4},{8,6},{10,8},{12,10},{14,12},{16,14},{18,... | collective-permute-start | bytes 6152 | tf_op jit(solution)/shard_map/ppermute | solution.py:58
  35.4 10.5 %collective-permute-start.4 = (f32[8,64]{1,0:T(8,128)S(1)}, f32[8,64]{1,0:T(8,128)S(1)}, u32[]{:S(2)}, u32[]{:S(2)}) collective-permute-start(f32[8,64]{1,0:T(8,128)S(1)} %collective-permute-done.3), channel_id=1, source_target_pairs={{0,2},{2,4},{4,6},{6,8},{8,10},{10,12},{12,14},{14,16},{16,18},{18... | collective-permute-start | bytes 6152 | tf_op jit(solution)/shard_map/ppermute | solution.py:56
  42.4 9.2 %copy-start.6 = (f32[8,128]{1,0:T(8,128)S(1)}, f32[8,128]{1,0:T(8,128)}, u32[]{:S(2)}) copy-start(f32[8,128]{1,0:T(8,128)} %param.7) | copy-start | bytes 12292
  42.4 4.8 %collective-permute-start.12 = (f32[8,64]{1,0:T(8,128)S(1)}, f32[8,64]{1,0:T(8,128)S(1)}, u32[]{:S(2)}, u32[]{:S(2)}) collective-permute-start(f32[8,64]{1,0:T(8,128)S(1)} %collective-permute-done.11), channel_id=1, source_target_pairs={{0,30},{2,0},{4,2},{6,4},{8,6},{10,8},{12,10},{14,12},{16,14},{18,... | collective-permute-start | bytes 6152 | tf_op jit(solution)/shard_map/ppermute | solution.py:58
  45.9 5.7 %collective-permute-start.5 = (f32[8,64]{1,0:T(8,128)S(1)}, f32[8,64]{1,0:T(8,128)S(1)}, u32[]{:S(2)}, u32[]{:S(2)}) collective-permute-start(f32[8,64]{1,0:T(8,128)S(1)} %collective-permute-done.4), channel_id=1, source_target_pairs={{0,2},{2,4},{4,6},{6,8},{8,10},{10,12},{12,14},{14,16},{16,18},{18... | collective-permute-start | bytes 6152 | tf_op jit(solution)/shard_map/ppermute | solution.py:56
  47.2 5.7 %collective-permute-start.13 = (f32[8,64]{1,0:T(8,128)S(1)}, f32[8,64]{1,0:T(8,128)S(1)}, u32[]{:S(2)}, u32[]{:S(2)}) collective-permute-start(f32[8,64]{1,0:T(8,128)S(1)} %collective-permute-done.12), channel_id=1, source_target_pairs={{0,30},{2,0},{4,2},{6,4},{8,6},{10,8},{12,10},{14,12},{16,14},{18,... | collective-permute-start | bytes 6152 | tf_op jit(solution)/shard_map/ppermute | solution.py:58
  51.6 5.7 %collective-permute-start.6 = (f32[8,64]{1,0:T(8,128)S(1)}, f32[8,64]{1,0:T(8,128)S(1)}, u32[]{:S(2)}, u32[]{:S(2)}) collective-permute-start(f32[8,64]{1,0:T(8,128)S(1)} %collective-permute-done.5), channel_id=1, source_target_pairs={{0,2},{2,4},{4,6},{6,8},{8,10},{10,12},{12,14},{14,16},{16,18},{18... | collective-permute-start | bytes 6152 | tf_op jit(solution)/shard_map/ppermute | solution.py:56
  53.0 23.2 %collective-permute-start.14 = (f32[8,64]{1,0:T(8,128)S(1)}, f32[8,64]{1,0:T(8,128)S(1)}, u32[]{:S(2)}, u32[]{:S(2)}) collective-permute-start(f32[8,64]{1,0:T(8,128)S(1)} %collective-permute-done.13), channel_id=1, source_target_pairs={{0,30},{2,0},{4,2},{6,4},{8,6},{10,8},{12,10},{14,12},{16,14},{18,... | collective-permute-start | bytes 6152 | tf_op jit(solution)/shard_map/ppermute | solution.py:58
  57.4 18.8 %collective-permute-start.7 = (f32[8,64]{1,0:T(8,128)S(1)}, f32[8,64]{1,0:T(8,128)S(1)}, u32[]{:S(2)}, u32[]{:S(2)}) collective-permute-start(f32[8,64]{1,0:T(8,128)S(1)} %collective-permute-done.6), channel_id=1, source_target_pairs={{0,2},{2,4},{4,6},{6,8},{8,10},{10,12},{12,14},{14,16},{16,18},{18... | collective-permute-start | bytes 6152 | tf_op jit(solution)/shard_map/ppermute | solution.py:56
  78.4 0.7 copy-start.5
  78.4 118.7 %reduce-scatter.6.cloned.1.call-start = ((), (), s32[]{:S(2)}) async-start(), calls=%async_computation.4 | async-start | bytes 98304 | tf_op jit(solution)/shard_map/reduce_scatter | solution.py:90
  86.7 40.2 %copy-start.1 = (f32[64,64]{1,0:T(8,128)S(1)}, f32[64,64]{1,0:T(8,128)}, u32[]{:S(2)}) copy-start(f32[64,64]{1,0:T(8,128)} %reduce-scatter.4.cloned.1.call-done) | copy-start | bytes 49156
  190.6 109.2 %reduce-scatter.8.cloned.1.call-start = ((), (), s32[]{:S(2)}) async-start(), calls=%async_computation.5 | async-start | bytes 278528 | tf_op jit(solution)/shard_map/reduce_scatter | solution.py:104
Sparse Core Ops, SparseCore 0:
  78.5 8.0 reduce-scatter.3
  190.7 6.2 reduce-scatter.5
  243.5 56.2 reduce-scatter.7
